TPU v7x, 32 devices: a whole 2x2x4 slice. The times are simulated.
32 devices in a mesh: pipe: 2 (over x), expert: 16 (over z, y, core).
Axes of the slice: x: 2, y: 2, z: 4, core: 2. Of those that a mesh axis runs over, the one named last changes fastest.
Arguments:
- front_tokens: bfloat16 [2, 192, 3584], P('pipe', 'expert'), may hold values from -6 to 6
- front_routes: int32 [2, 192, 2], P('pipe', 'expert'), may hold values from 0 to 1, all different within a row; in each aligned block of 12 rows (0 to 11, 12 to 23, ..., all dimensions but the last counted through in order) at most 12 rows name the same one
- front_mixing: int32 [2, 192, 2], P('pipe', 'expert'), may hold values from 1 to 15
- back_tokens: bfloat16 [2, 192, 3584], P('pipe', 'expert'), may hold values from -6 to 6
- back_routes: int32 [2, 192, 2], P('pipe', 'expert'), may hold values from 0 to 1, all different within a row; in each aligned block of 12 rows (0 to 11, 12 to 23, ..., all dimensions but the last counted through in order) at most 12 rows name the same one
- back_mixing: int32 [2, 192, 2], P('pipe', 'expert'), may hold values from 1 to 15
- back_upstream: bfloat16 [2, 192, 3584], P('pipe', 'expert'), may hold values from -6 to 6
- gate_weight: bfloat16 [2, 3584, 2048], P('pipe', None, 'expert'), may hold values from -0.09375 to 0.09375
- up_weight: bfloat16 [2, 3584, 2048], P('pipe', None, 'expert'), may hold values from -0.09375 to 0.09375
- down_weight: bfloat16 [2, 2048, 3584], P('pipe', 'expert'), may hold values from -0.1875 to 0.1875
Outputs:
- front_result: bfloat16 [2, 192, 3584], P('pipe', 'expert')
- token_grads: bfloat16 [2, 192, 3584], P('pipe', 'expert')
- gate_grads: bfloat16 [2, 1792, 2048], P('pipe', None, 'expert')
- up_grads: bfloat16 [2, 1792, 2048], P('pipe', None, 'expert')
- down_grads: bfloat16 [2, 2048, 1792], P('pipe', 'expert')
Inputs may be any that keep to these rules, and one draw needn't show every extreme that they name: `front_routes`: each row names 2 different experts; within each device's block of 12 rows no expert is named more than 12 times, a bound that some block reaches. `back_routes`: each row names 2 different experts; within each device's block of 12 rows no expert is named more than 12 times, a bound that some block reaches.
All inputs are finite; a program needn't handle non-finite values.
Results may differ from a plain program's by a relative error of at most 0.0071.
Values may be sent and summed in bfloat16 or wider, within the bound.
A program may use at most 64 MiB of HBM per device.

v0:
```python
import jax
import jax.numpy as jnp
from jax import lax
from jax.sharding import PartitionSpec as P

SHARDS = 8
weight_unit = 0.0625


def hit_tables(routes, mixing, experts, capacity):
    token_count, route_count = routes.shape
    flat_routes = routes.reshape(token_count * route_count)
    matches = (flat_routes[:, None] == jnp.arange(experts, dtype=jnp.int32)[None, :]).astype(
        jnp.int32
    )
    earlier = jnp.cumsum(matches, axis=0) - matches
    position = jnp.sum(earlier * matches, axis=1)
    slot_ids = flat_routes * capacity + position
    hit_table = (
        slot_ids[:, None] == jnp.arange(experts * capacity, dtype=jnp.int32)[None, :]
    ).astype(jnp.float32)
    hit_table = hit_table.reshape(token_count, route_count, experts * capacity)
    weights = mixing.astype(jnp.float32) * weight_unit
    picker = jnp.sum(hit_table, axis=1)
    mix_table = jnp.sum(hit_table * weights[:, :, None], axis=1)
    return (picker, mix_table)


def deliver(slot_rows, experts, capacity):
    stacks = slot_rows.shape[0]
    feature_count = slot_rows.shape[2]
    copies = jnp.repeat(slot_rows.reshape(stacks, experts, capacity, feature_count), SHARDS, axis=1)
    landed = lax.all_to_all(copies, "expert", split_axis=1, concat_axis=1, tiled=True)
    return landed.reshape(stacks, experts * SHARDS * capacity, feature_count)


def collect(shard_parts, experts, capacity):
    feature_count = shard_parts.shape[1]
    sources = experts * SHARDS
    returned = lax.all_to_all(
        shard_parts.reshape(sources, capacity, feature_count),
        "expert",
        split_axis=0,
        concat_axis=0,
        tiled=True,
    )
    summed = jnp.sum(
        returned.reshape(experts, SHARDS, capacity, feature_count).astype(jnp.float32), axis=1
    )
    result_rows = summed.astype(jnp.bfloat16).reshape(experts * capacity, feature_count)
    return result_rows


def mirror_move(values, split_dim, concat_dim):
    return lax.all_to_all(values, "pipe", split_axis=split_dim, concat_axis=concat_dim, tiled=True)


def local(
    front_tokens,
    front_routes,
    front_mixing,
    back_tokens,
    back_routes,
    back_mixing,
    back_upstream,
    gate_weight,
    up_weight,
    down_weight,
):
    experts = lax.axis_size("expert") // SHARDS
    token_count = front_tokens.shape[1]
    route_count = front_routes.shape[2]
    feature_count = front_tokens.shape[2]
    capacity = min(token_count, max(2, 3 * token_count * route_count // (2 * experts)))
    front_pick, front_mix = hit_tables(front_routes[0], front_mixing[0], experts, capacity)
    back_pick, back_mix = hit_tables(back_routes[0], back_mixing[0], experts, capacity)
    front_slots = jnp.dot(
        front_pick.T.astype(jnp.bfloat16), front_tokens[0], preferred_element_type=jnp.float32
    ).astype(jnp.bfloat16)
    back_slots = jnp.dot(
        back_pick.T.astype(jnp.bfloat16), back_tokens[0], preferred_element_type=jnp.float32
    ).astype(jnp.bfloat16)
    scaled_slots = jnp.dot(
        back_mix.T, back_upstream[0].astype(jnp.float32), precision=lax.Precision.HIGHEST
    ).astype(jnp.bfloat16)
    landed = deliver(jnp.stack([front_slots, back_slots, scaled_slots]), experts, capacity)
    gate_cols = gate_weight[0]
    up_cols = up_weight[0]
    down_rows = down_weight[0]
    front_rows = landed[0]
    front_gate = jnp.dot(front_rows, gate_cols, preferred_element_type=jnp.float32)
    front_up = jnp.dot(front_rows, up_cols, preferred_element_type=jnp.float32)
    front_hidden = (jax.nn.silu(front_gate) * front_up).astype(jnp.bfloat16)
    front_parts = jnp.dot(front_hidden, down_rows, preferred_element_type=jnp.float32).astype(
        jnp.bfloat16
    )
    front_summed = collect(front_parts, experts, capacity)
    front_result = jnp.dot(
        front_mix, front_summed.astype(jnp.float32), precision=lax.Precision.HIGHEST
    ).astype(jnp.bfloat16)
    back_rows = landed[1]
    scaled_rows = landed[2]
    back_gate = jnp.dot(back_rows, gate_cols, preferred_element_type=jnp.float32)
    back_up = jnp.dot(back_rows, up_cols, preferred_element_type=jnp.float32)
    gate_act = jax.nn.silu(back_gate)
    gate_sig = jax.nn.sigmoid(back_gate)
    back_hidden = (gate_act * back_up).astype(jnp.bfloat16)
    down_section = jnp.dot(scaled_rows.T, back_hidden, preferred_element_type=jnp.float32).astype(
        jnp.bfloat16
    )
    hidden_grad = jnp.dot(scaled_rows, down_rows.T, preferred_element_type=jnp.float32)
    act_slope = gate_sig * (1.0 + back_gate * (1.0 - gate_sig))
    gate_delta = (hidden_grad * back_up * act_slope).astype(jnp.bfloat16)
    up_delta = (hidden_grad * gate_act).astype(jnp.bfloat16)
    gate_section = jnp.dot(back_rows.T, gate_delta, preferred_element_type=jnp.float32).astype(
        jnp.bfloat16
    )
    up_section = jnp.dot(back_rows.T, up_delta, preferred_element_type=jnp.float32).astype(
        jnp.bfloat16
    )
    back_parts = (
        jnp.dot(gate_delta, gate_cols.T, preferred_element_type=jnp.float32)
        + jnp.dot(up_delta, up_cols.T, preferred_element_type=jnp.float32)
    ).astype(jnp.bfloat16)
    grad_slots = collect(back_parts, experts, capacity)
    token_grads = jnp.dot(
        back_pick.astype(jnp.bfloat16), grad_slots, preferred_element_type=jnp.float32
    ).astype(jnp.bfloat16)
    section_grads = lax.optimization_barrier(jnp.stack([gate_section, up_section, down_section]))
    pipe_count = lax.axis_size("pipe")
    half_rows = feature_count // 2
    upper_half = lax.axis_index("pipe") * 2 >= pipe_count
    own_half = jnp.where(upper_half, section_grads[:, half_rows:], section_grads[:, :half_rows])
    leaving = jnp.where(upper_half, section_grads[:, :half_rows], section_grads[:, half_rows:])
    piece_rows = half_rows // pipe_count
    spread_out = mirror_move(leaving, 1, 0)
    by_source = spread_out.reshape(pipe_count, 3, piece_rows, leaving.shape[2])
    reversed_sources = jnp.flip(by_source, axis=0).reshape(
        pipe_count * 3, piece_rows, leaving.shape[2]
    )
    leaving = mirror_move(reversed_sources, 0, 1)
    summed = (own_half.astype(jnp.float32) + leaving.astype(jnp.float32)).astype(jnp.bfloat16)
    return (
        front_result[None],
        token_grads[None],
        summed[0][None],
        summed[1][None],
        summed[2].T[None],
    )


def solution(mesh):
    placed = (
        P("pipe", "expert", None),
        P("pipe", "expert", None),
        P("pipe", "expert", None),
        P("pipe", "expert", None),
        P("pipe", "expert", None),
        P("pipe", "expert", None),
        P("pipe", "expert", None),
        P("pipe", None, "expert"),
        P("pipe", None, "expert"),
        P("pipe", "expert", None),
    )
    return jax.shard_map(
        local,
        mesh=mesh,
        in_specs=placed,
        out_specs=(
            P("pipe", "expert", None),
            P("pipe", "expert", None),
            P("pipe", None, "expert"),
            P("pipe", None, "expert"),
            P("pipe", "expert", None),
        ),
        check_vma=False,
    )
```

profile of v0, /device:TPU:13, one launch (start us, length us, event | category | flops | bytes accessed | tf_op | source)
XLA Modules:
  0.0 313.1 jit_solution(14618682792077326766)
XLA Ops:
  0.7 0.9 copy.61
  2.1 0.7 bitcast_add_fusion.2
  2.9 0.7 multiply_bitcast_fusion.1
  3.7 0.8 copy.65
  5.0 0.7 bitcast_add_fusion.1
  5.8 0.7 multiply_bitcast_fusion
  6.7 1.2 convolution_convert_fusion.4
  8.0 1.1 convolution_convert_fusion.5
  9.8 3.1 broadcast_in_dim.8
  12.9 6.6 %all-to-all-start = ((bf16[3,16,12,3584]{3,2,0,1:T(8,128)(2,1)}), bf16[3,16,12,3584]{3,2,0,1:T(8,128)(2,1)}, u32[]{:S(2)}, u32[]{:S(2)}) async-start(bf16[3,16,12,3584]{3,2,0,1:T(8,128)(2,1)} %bitcast.97), calls=%async_computation | async-start | bytes 11010048 | tf_op jit(solution)/shard_map/all_to_all | solution.py:33
  19.4 120.6 %all-to-all-done = bf16[3,16,12,3584]{3,2,0,1:T(8,128)(2,1)} async-done(((bf16[3,16,12,3584]{3,2,0,1:T(8,128)(2,1)}), bf16[3,16,12,3584]{3,2,0,1:T(8,128)(2,1)}, u32[]{:S(2)}, u32[]{:S(2)}) %all-to-all-start) | async-done | bytes 4128800 | tf_op jit(solution)/shard_map/all_to_all | solution.py:33
  140.0 5.2 %fusion.40 = (bf16[1,16,12,3584]{3,2,0,1:T(8,128)(2,1)}, bf16[1,16,12,3584]{3,2,0,1:T(8,128)(2,1)}, bf16[1,16,12,3584]{3,2,0,1:T(8,128)(2,1)}) fusion(bf16[3,16,12,3584]{3,2,0,1:T(8,128)(2,1)} %all-to-all-done), kind=kLoop, calls=%fused_computation.75 | loop fusion | bytes 8257536 | tf_op jit(solution)/shard_map/slice | solution.py:102
  145.2 2.4 squeeze.40
  147.6 0.5 fusion.18
  148.1 0.5 fusion.12
  148.7 3.4 %squeeze.39 = bf16[192,3584]{1,0:T(8,128)(2,1)} reshape(bf16[1,16,12,3584]{3,2,0,1:T(8,128)(2,1)} %get-tuple-element.34) | data formatting | bytes 2752512 | tf_op jit(solution)/shard_map/squeeze | solution.py:102
  152.1 2.2 fusion.3
  154.3 0.5 multiply_convert_fusion.1
  154.8 0.7 fusion.2
  155.5 0.7 fusion.1
  156.3 0.3 pad_maximum_fusion
  156.7 1.4 copy-done.1
  158.1 8.5 %copy.70 = bf16[3,1792,128]{2,0,1:T(4,128)(2,1)S(1)} copy(bf16[3,1792,128]{2,1,0:T(8,128)(2,1)S(1)} %broadcast_select_fusion) | data formatting | bytes 2752512 | tf_op jit(solution)/shard_map/jit(_where)/select_n | solution.py:134
  166.6 24.4 %all_to_all.39 = bf16[3,1792,128]{2,0,1:T(4,128)(2,1)S(1)} all-to-all(bf16[3,1792,128]{2,0,1:T(4,128)(2,1)S(1)} %copy.70), channel_id=1, replica_groups=mesh['pipe'=2,'expert'=16] {'pipe'}, dimensions={1} | all-to-all | bytes 2752512 | tf_op jit(solution)/shard_map/all_to_all | solution.py:55
  191.3 1.2 reverse.3
  192.5 2.5 copy.72
  195.0 4.8 %all-to-all-start.4 = ((bf16[6,896,128]{2,1,0:T(8,128)(2,1)}), bf16[6,896,128]{2,1,0:T(8,128)(2,1)}, u32[]{:S(2)}, u32[]{:S(2)}) async-start(bf16[6,896,128]{2,1,0:T(8,128)(2,1)} %bitcast.20), calls=%async_computation.4 | async-start | bytes 2752512 | tf_op jit(solution)/shard_map/all_to_all | solution.py:55
  199.7 2.4 squeeze.35
  202.1 0.5 fusion.20
  202.6 3.2 %convolution_convert_fusion = bf16[192,3584]{1,0:T(8,128)(2,1)} fusion(bf16[192,3584]{1,0:T(8,128)(2,1)S(1)} %squeeze.35, bf16[1,128,3584]{2,1,0:T(8,128)(2,1)} %param.19, bf16[1,3584,128]{2,1,0:T(8,128)(2,1)S(1)} %copy-done, f32[192,128]{1,0:T(8,128)S(1)} %fusion.20), kind=kOutput, calls=%fused_computation.2 | convolution fusion | flops 353157120 | bytes 4685824 | tf_op jit(solution)/shard_map/dot_general | solution.py:94
  205.9 3.3 %reshape.117 = bf16[16,12,3584]{2,1,0:T(8,128)(2,1)} reshape(bf16[192,3584]{1,0:T(8,128)(2,1)} %convolution_convert_fusion) | data formatting | bytes 2752512 | tf_op jit(solution)/shard_map/reshape | solution.py:41
  209.1 6.6 %all-to-all-done.4 = bf16[6,896,128]{2,1,0:T(8,128)(2,1)} async-done(((bf16[6,896,128]{2,1,0:T(8,128)(2,1)}), bf16[6,896,128]{2,1,0:T(8,128)(2,1)}, u32[]{:S(2)}, u32[]{:S(2)}) %all-to-all-start.4) | async-done | bytes 1376288 | tf_op jit(solution)/shard_map/all_to_all | solution.py:55
  215.7 6.7 %all-to-all-start.1 = ((bf16[16,12,3584]{2,1,0:T(8,128)(2,1)}), bf16[16,12,3584]{2,1,0:T(8,128)(2,1)}, u32[]{:S(2)}, u32[]{:S(2)}) async-start(bf16[16,12,3584]{2,1,0:T(8,128)(2,1)} %reshape.117), calls=%async_computation.1 | async-start | bytes 3670016 | tf_op jit(solution)/shard_map/all_to_all | solution.py:40
  222.4 0.5 fusion.16
  222.9 0.5 fusion
  223.5 1.4 reshape.120
  224.9 39.4 %all-to-all-done.1 = bf16[16,12,3584]{2,1,0:T(8,128)(2,1)} async-done(((bf16[16,12,3584]{2,1,0:T(8,128)(2,1)}), bf16[16,12,3584]{2,1,0:T(8,128)(2,1)}, u32[]{:S(2)}, u32[]{:S(2)}) %all-to-all-start.1) | async-done | bytes 1376288 | tf_op jit(solution)/shard_map/all_to_all | solution.py:40
  264.3 4.9 %all-to-all-start.2 = ((bf16[16,12,3584]{2,1,0:T(8,128)(2,1)}), bf16[16,12,3584]{2,1,0:T(8,128)(2,1)S(1)}, u32[]{:S(2)}, u32[]{:S(2)}) async-start(bf16[16,12,3584]{2,1,0:T(8,128)(2,1)} %reshape.120), calls=%async_computation.2 | async-start | bytes 3670016 | tf_op jit(solution)/shard_map/all_to_all | solution.py:40
  269.2 1.5 convert_bitcast_fusion
  271.0 1.6 copy-done.2
  272.5 0.4 fusion.6
  273.0 1.0 slice_bitcast_fusion
  274.0 1.0 copy.74
  275.0 1.8 bitcast_reduce_fusion.1
  276.8 34.2 %all-to-all-done.2 = bf16[16,12,3584]{2,1,0:T(8,128)(2,1)S(1)} async-done(((bf16[16,12,3584]{2,1,0:T(8,128)(2,1)}), bf16[16,12,3584]{2,1,0:T(8,128)(2,1)S(1)}, u32[]{:S(2)}, u32[]{:S(2)}) %all-to-all-start.2) | async-done | bytes 1376288 | tf_op jit(solution)/shard_map/all_to_all | solution.py:40
  311.0 0.3 bitcast_reduce_fusion
  311.4 0.8 fusion.5
  312.2 0.9 fusion.4
  (41 shorter events, 2.9 us)
Async XLA Ops:
  0.6 147.5 %copy-start = (bf16[1,3584,128]{2,1,0:T(8,128)(2,1)S(1)}, bf16[1,3584,128]{2,1,0:T(8,128)(2,1)}, u32[]{:S(2)}) copy-start(bf16[1,3584,128]{2,1,0:T(8,128)(2,1)} %param.18) | copy-start | bytes 2752516
  0.6 8.7 %copy-start.6 = (bf16[1,12,3584]{2,1,0:T(8,128)(2,1)S(1)}, bf16[1,12,3584]{2,1,0:T(8,128)(2,1)}, u32[]{:S(2)}) copy-start(bf16[1,12,3584]{2,1,0:T(8,128)(2,1)} %param.10) | copy-start | bytes 258052
  12.9 127.1 %all-to-all-start = ((bf16[3,16,12,3584]{3,2,0,1:T(8,128)(2,1)}), bf16[3,16,12,3584]{3,2,0,1:T(8,128)(2,1)}, u32[]{:S(2)}, u32[]{:S(2)}) async-start(bf16[3,16,12,3584]{3,2,0,1:T(8,128)(2,1)} %bitcast.97), calls=%async_computation | async-start | bytes 11010048 | tf_op jit(solution)/shard_map/all_to_all | solution.py:33
  145.2 2.5 copy-start.3
  152.1 2.2 copy-start.4
  152.1 2.2 copy-start.5
  156.6 1.6 copy-start.1
  195.0 20.8 %all-to-all-start.4 = ((bf16[6,896,128]{2,1,0:T(8,128)(2,1)}), bf16[6,896,128]{2,1,0:T(8,128)(2,1)}, u32[]{:S(2)}, u32[]{:S(2)}) async-start(bf16[6,896,128]{2,1,0:T(8,128)(2,1)} %bitcast.20), calls=%async_computation.4 | async-start | bytes 2752512 | tf_op jit(solution)/shard_map/all_to_all | solution.py:55
  215.7 48.6 %all-to-all-start.1 = ((bf16[16,12,3584]{2,1,0:T(8,128)(2,1)}), bf16[16,12,3584]{2,1,0:T(8,128)(2,1)}, u32[]{:S(2)}, u32[]{:S(2)}) async-start(bf16[16,12,3584]{2,1,0:T(8,128)(2,1)} %reshape.117), calls=%async_computation.1 | async-start | bytes 3670016 | tf_op jit(solution)/shard_map/all_to_all | solution.py:40
  264.3 46.7 %all-to-all-start.2 = ((bf16[16,12,3584]{2,1,0:T(8,128)(2,1)}), bf16[16,12,3584]{2,1,0:T(8,128)(2,1)S(1)}, u32[]{:S(2)}, u32[]{:S(2)}) async-start(bf16[16,12,3584]{2,1,0:T(8,128)(2,1)} %reshape.120), calls=%async_computation.2 | async-start | bytes 3670016 | tf_op jit(solution)/shard_map/all_to_all | solution.py:40
  270.8 1.8 copy-start.2
where the time goes:
time: 314 us; the launch traced here: 313 us
  waiting for transfers between devices  201 us (64%)
  local copies, waits for them, and re-layouts  41.6 us (13%)
  blocking collectives  24.4 us (8%)
  starting transfers between devices  22.9 us (7%)
  matrix products  14.2 us (5%)
  other arithmetic  8.21 us (3%)
    all_to_all x1, waiting for transfers between devices, deliver(): lax.all_to_all(copies, 'expert', split_axis=1, concat_axis=1, tiled=True)  121 us
    all_to_all x2, waiting for transfers between devices, collect(): lax.all_to_all(shard_parts.reshape(sources, capacity, feature_count), 'ex...  73.6 us
    all_to_all x1, blocking collectives, mirror_move(): lax.all_to_all(values, 'pipe', split_axis=split_dim, concat_axis=concat_d...  24.4 us
    all_to_all x2, starting transfers between devices, collect(): lax.all_to_all(shard_parts.reshape(sources, capacity, feature_count), 'ex...  11.6 us
    select_n x1, local copies, waits for them, and re-layouts, local(): jnp.where(upper_half, section_grads[:, :half_rows], section_grads[:, half...  8.52 us
    all_to_all x1, waiting for transfers between devices, mirror_move(): lax.all_to_all(values, 'pipe', split_axis=split_dim, concat_axis=concat_d...  6.6 us
    all_to_all x1, starting transfers between devices, deliver(): lax.all_to_all(copies, 'expert', split_axis=1, concat_axis=1, tiled=True)  6.55 us
  transfers between devices with their start and end apart: 4, of which 4 were waited for; matrix products, arithmetic and copies ran while one was open for 6% of the time, Pallas kernels for 0%

commit v1 on v0

--- a/solution.py
+++ b/solution.py
@@ -5,6 +5,22 @@
 
 SHARDS = 8
 weight_unit = 0.0625
+
+
+def exchange_in_pairs(x, axis, split, join):
+    ways, here = (lax.axis_size(axis), lax.axis_index(axis))
+    width = x.shape[split] // ways
+    lengths = list(x.shape)
+    lengths[split] = width
+    height = lengths[join]
+    lengths[join] = height * ways
+    full = jnp.zeros(lengths, x.dtype)
+    for mask in range(ways):
+        part = lax.dynamic_slice_in_dim(x, (here ^ mask) * width, width, axis=split)
+        if mask:
+            part = lax.ppermute(part, axis, [(d, d ^ mask) for d in range(ways)])
+        full = lax.dynamic_update_slice_in_dim(full, part, (here ^ mask) * height, axis=join)
+    return full
 
 
 def hit_tables(routes, mixing, experts, capacity):
@@ -30,7 +46,7 @@
     stacks = slot_rows.shape[0]
     feature_count = slot_rows.shape[2]
     copies = jnp.repeat(slot_rows.reshape(stacks, experts, capacity, feature_count), SHARDS, axis=1)
-    landed = lax.all_to_all(copies, "expert", split_axis=1, concat_axis=1, tiled=True)
+    landed = exchange_in_pairs(copies, "expert", 1, 1)
     return landed.reshape(stacks, experts * SHARDS * capacity, feature_count)
 
 

time: 314 us -> 344 us (1.096)
  starting transfers between devices: 22.9 us -> 56.5 us
  waiting for transfers between devices: 201 us -> 183 us
  local copies, waits for them, and re-layouts: 41.6 us -> 56.7 us
    all_to_all x1 -> x0, waiting for transfers between devices: 121 us -> none  [deliver(): lax.all_to_all(copies, 'expert', split_axis=1, concat_axis=1, tiled=True)]
    ppermute x0 -> x15, waiting for transfers between devices: none -> 103 us  [exchange_in_pairs(): part = lax.ppermute(part, axis, [(d, d ^ mask) for d in range(ways)])]
    ppermute x0 -> x15, starting transfers between devices: none -> 38.2 us  [exchange_in_pairs(): part = lax.ppermute(part, axis, [(d, d ^ mask) for d in range(ways)])]
    dynamic_update_slice x0 -> x15, local copies, waits for them, and re-layouts: none -> 16.4 us  [exchange_in_pairs(): lax.dynamic_update_slice_in_dim(full, part, (here ^ mask) * height, axis=...]
    all_to_all x1 -> x0, starting transfers between devices: 6.55 us -> none  [deliver(): lax.all_to_all(copies, 'expert', split_axis=1, concat_axis=1, tiled=True)]
  transfers between devices with their start and end apart: 4 -> 18, of which waited for: 4 -> 13; matrix products, arithmetic and copies ran while one was open for 6% -> 9% of each run, Pallas kernels for 0% -> 0%
where the time goes in v1:
time: 344 us; the launch traced here: 343 us
  waiting for transfers between devices  183 us (53%)
  local copies, waits for them, and re-layouts  56.7 us (16%)
  starting transfers between devices  56.5 us (16%)
  blocking collectives  24.3 us (7%)
  matrix products  13.6 us (4%)
  other arithmetic  8.08 us (2%)
    ppermute x15, waiting for transfers between devices, exchange_in_pairs(): part = lax.ppermute(part, axis, [(d, d ^ mask) for d in range(ways)])  103 us
    all_to_all x2, waiting for transfers between devices, collect(): lax.all_to_all(shard_parts.reshape(sources, capacity, feature_count), 'ex...  73.6 us
    ppermute x15, starting transfers between devices, exchange_in_pairs(): part = lax.ppermute(part, axis, [(d, d ^ mask) for d in range(ways)])  38.2 us
    all_to_all x1, blocking collectives, mirror_move(): lax.all_to_all(values, 'pipe', split_axis=split_dim, concat_axis=concat_d...  24.3 us
    dynamic_update_slice x15, local copies, waits for them, and re-layouts, exchange_in_pairs(): lax.dynamic_update_slice_in_dim(full, part, (here ^ mask) * height, axis=...  16.4 us
    all_to_all x2, starting transfers between devices, collect(): lax.all_to_all(shard_parts.reshape(sources, capacity, feature_count), 'ex...  13.7 us
    select_n x1, local copies, waits for them, and re-layouts, local(): jnp.where(upper_half, section_grads[:, :half_rows], section_grads[:, half...  8.54 us
  transfers between devices with their start and end apart: 18, of which 13 were waited for; matrix products, arithmetic and copies ran while one was open for 9% of the time, Pallas kernels for 0%

profile of v1, /device:TPU:13, one launch (start us, length us, event | category | flops | bytes accessed | tf_op | source)
XLA Modules:
  0.0 343.1 jit_solution(3515583153434652443)
XLA Ops:
  6.5 1.2 convolution_convert_fusion.4
  7.9 1.1 convolution_convert_fusion.6
  9.1 1.1 convolution_convert_fusion.5
  11.8 1.7 constant_dynamic-slice_fusion
  13.6 2.4 copy-done.3
  16.7 1.1 collective-permute-start.14
  18.9 2.0 collective-permute-start.12
  21.4 1.8 constant_dynamic-update-slice_fusion.13
  23.1 7.7 %collective-permute-done.1 = bf16[3,1,12,3584]{3,2,1,0:T(8,128)(2,1)S(1)} collective-permute-done((bf16[3,1,12,3584]{3,2,1,0:T(8,128)(2,1)}, bf16[3,1,12,3584]{3,2,1,0:T(8,128)(2,1)S(1)}, u32[]{:S(2)}, u32[]{:S(2)}) %collective-permute-start.1) | collective-permute-done | bytes 258080 | tf_op jit(solution)/shard_map/ppermute | solution.py:21
  32.7 8.9 %collective-permute-done.2 = bf16[3,1,12,3584]{3,2,1,0:T(8,128)(2,1)S(1)} collective-permute-done((bf16[3,1,12,3584]{3,2,1,0:T(8,128)(2,1)}, bf16[3,1,12,3584]{3,2,1,0:T(8,128)(2,1)S(1)}, u32[]{:S(2)}, u32[]{:S(2)}) %collective-permute-start.2) | collective-permute-done | bytes 258080 | tf_op jit(solution)/shard_map/ppermute | solution.py:21
  41.6 13.1 %collective-permute-start.3 = (bf16[3,1,12,3584]{3,2,1,0:T(8,128)(2,1)}, bf16[3,1,12,3584]{3,2,1,0:T(8,128)(2,1)S(1)}, u32[]{:S(2)}, u32[]{:S(2)}) collective-permute-start(bf16[3,1,12,3584]{3,2,1,0:T(8,128)(2,1)} %get-tuple-element.48), channel_id=1, source_target_pairs={{0,4},{1,5},{2,6},{3,7},{4,0},{5,1},{6,2},{7,3},{8,12},{9,13},{10,... | collective-permute-start | bytes 774152 | tf_op jit(solution)/shard_map/ppermute | solution.py:21
  55.4 7.7 %collective-permute-done.3 = bf16[3,1,12,3584]{3,2,1,0:T(8,128)(2,1)S(1)} collective-permute-done((bf16[3,1,12,3584]{3,2,1,0:T(8,128)(2,1)}, bf16[3,1,12,3584]{3,2,1,0:T(8,128)(2,1)S(1)}, u32[]{:S(2)}, u32[]{:S(2)}) %collective-permute-start.3) | collective-permute-done | bytes 258080 | tf_op jit(solution)/shard_map/ppermute | solution.py:21
  63.1 2.1 collective-permute-start.4
  66.0 8.2 %collective-permute-done.4 = bf16[3,1,12,3584]{3,2,1,0:T(8,128)(2,1)S(1)} collective-permute-done((bf16[3,1,12,3584]{3,2,1,0:T(8,128)(2,1)}, bf16[3,1,12,3584]{3,2,1,0:T(8,128)(2,1)S(1)}, u32[]{:S(2)}, u32[]{:S(2)}) %collective-permute-start.4) | collective-permute-done | bytes 258080 | tf_op jit(solution)/shard_map/ppermute | solution.py:21
  75.5 9.2 %collective-permute-done.5 = bf16[3,1,12,3584]{3,2,1,0:T(8,128)(2,1)S(1)} collective-permute-done((bf16[3,1,12,3584]{3,2,1,0:T(8,128)(2,1)S(1)}, bf16[3,1,12,3584]{3,2,1,0:T(8,128)(2,1)S(1)}, u32[]{:S(2)}, u32[]{:S(2)}) %collective-permute-start.5) | collective-permute-done | bytes 258080 | tf_op jit(solution)/shard_map/ppermute | solution.py:21
  84.8 1.3 collective-permute-start.6
  86.8 9.4 %collective-permute-done.6 = bf16[3,1,12,3584]{3,2,1,0:T(8,128)(2,1)S(1)} collective-permute-done((bf16[3,1,12,3584]{3,2,1,0:T(8,128)(2,1)S(1)}, bf16[3,1,12,3584]{3,2,1,0:T(8,128)(2,1)S(1)}, u32[]{:S(2)}, u32[]{:S(2)}) %collective-permute-start.6) | collective-permute-done | bytes 258080 | tf_op jit(solution)/shard_map/ppermute | solution.py:21
  97.7 12.6 %collective-permute-done.7 = bf16[3,1,12,3584]{3,2,1,0:T(8,128)(2,1)S(1)} collective-permute-done((bf16[3,1,12,3584]{3,2,1,0:T(8,128)(2,1)S(1)}, bf16[3,1,12,3584]{3,2,1,0:T(8,128)(2,1)S(1)}, u32[]{:S(2)}, u32[]{:S(2)}) %collective-permute-start.7) | collective-permute-done | bytes 258080 | tf_op jit(solution)/shard_map/ppermute | solution.py:21
  110.3 5.3 %collective-permute-start.8 = (bf16[3,1,12,3584]{3,2,1,0:T(8,128)(2,1)S(1)}, bf16[3,1,12,3584]{3,2,1,0:T(8,128)(2,1)S(1)}, u32[]{:S(2)}, u32[]{:S(2)}) collective-permute-start(bf16[3,1,12,3584]{3,2,1,0:T(8,128)(2,1)S(1)} %get-tuple-element.43), channel_id=1, source_target_pairs={{0,9},{1,8},{2,11},{3,10},{4,13},{5,12},{6,15},{7,14},{8,1},{9,0},... | collective-permute-start | bytes 774152 | tf_op jit(solution)/shard_map/ppermute | solution.py:21
  116.4 12.8 %collective-permute-done.8 = bf16[3,1,12,3584]{3,2,1,0:T(8,128)(2,1)S(1)} collective-permute-done((bf16[3,1,12,3584]{3,2,1,0:T(8,128)(2,1)S(1)}, bf16[3,1,12,3584]{3,2,1,0:T(8,128)(2,1)S(1)}, u32[]{:S(2)}, u32[]{:S(2)}) %collective-permute-start.8) | collective-permute-done | bytes 258080 | tf_op jit(solution)/shard_map/ppermute | solution.py:21
  129.2 4.3 %collective-permute-start.9 = (bf16[3,1,12,3584]{3,2,1,0:T(8,128)(2,1)S(1)}, bf16[3,1,12,3584]{3,2,1,0:T(8,128)(2,1)S(1)}, u32[]{:S(2)}, u32[]{:S(2)}) collective-permute-start(bf16[3,1,12,3584]{3,2,1,0:T(8,128)(2,1)S(1)} %get-tuple-element.42), channel_id=1, source_target_pairs={{0,10},{1,11},{2,8},{3,9},{4,14},{5,15},{6,12},{7,13},{8,2},{9,3},... | collective-permute-start | bytes 774152 | tf_op jit(solution)/shard_map/ppermute | solution.py:21
  134.3 13.8 %collective-permute-done.9 = bf16[3,1,12,3584]{3,2,1,0:T(8,128)(2,1)S(1)} collective-permute-done((bf16[3,1,12,3584]{3,2,1,0:T(8,128)(2,1)S(1)}, bf16[3,1,12,3584]{3,2,1,0:T(8,128)(2,1)S(1)}, u32[]{:S(2)}, u32[]{:S(2)}) %collective-permute-start.9) | collective-permute-done | bytes 258080 | tf_op jit(solution)/shard_map/ppermute | solution.py:21
  148.1 4.4 %collective-permute-start.10 = (bf16[3,1,12,3584]{3,2,1,0:T(8,128)(2,1)S(1)}, bf16[3,1,12,3584]{3,2,1,0:T(8,128)(2,1)S(1)}, u32[]{:S(2)}, u32[]{:S(2)}) collective-permute-start(bf16[3,1,12,3584]{3,2,1,0:T(8,128)(2,1)S(1)} %get-tuple-element.41), channel_id=1, source_target_pairs={{0,11},{1,10},{2,9},{3,8},{4,15},{5,14},{6,13},{7,12},{8,3},{9,2},... | collective-permute-start | bytes 774152 | tf_op jit(solution)/shard_map/ppermute | solution.py:21
  153.2 12.4 %collective-permute-done.10 = bf16[3,1,12,3584]{3,2,1,0:T(8,128)(2,1)S(1)} collective-permute-done((bf16[3,1,12,3584]{3,2,1,0:T(8,128)(2,1)S(1)}, bf16[3,1,12,3584]{3,2,1,0:T(8,128)(2,1)S(1)}, u32[]{:S(2)}, u32[]{:S(2)}) %collective-permute-start.10) | collective-permute-done | bytes 258080 | tf_op jit(solution)/shard_map/ppermute | solution.py:21
  166.4 1.7 constant_dynamic-update-slice_fusion.2
  168.1 1.7 constant_dynamic-update-slice_fusion.1
  169.9 1.7 constant_dynamic-update-slice_fusion
  171.6 1.7 constant_dynamic-update-slice_fusion.14
  173.3 4.8 %fusion.38 = (bf16[1,16,12,3584]{3,2,1,0:T(8,128)(2,1)S(1)}, bf16[1,16,12,3584]{3,2,1,0:T(8,128)(2,1)}, bf16[1,16,12,3584]{3,2,1,0:T(8,128)(2,1)}) fusion(bf16[3,16,12,3584]{3,2,1,0:T(8,128)(2,1)} %constant_dynamic-update-slice_fusion.14), kind=kLoop, calls=%fused_computation.101 | loop fusion | bytes 8257536 | tf_op jit(solution)/shard_map/slice | solution.py:118
  178.1 1.3 squeeze.39
  179.4 2.4 squeeze.40
  186.3 8.5 %copy.67 = bf16[3,1792,128]{2,0,1:T(4,128)(2,1)S(1)} copy(bf16[3,1792,128]{2,1,0:T(8,128)(2,1)S(1)} %broadcast_select_fusion) | data formatting | bytes 2752512 | tf_op jit(solution)/shard_map/jit(_where)/select_n | solution.py:150
  194.9 24.3 %all_to_all.34 = bf16[3,1792,128]{2,0,1:T(4,128)(2,1)S(1)} all-to-all(bf16[3,1792,128]{2,0,1:T(4,128)(2,1)S(1)} %copy.67), channel_id=1, replica_groups=mesh['pipe'=2,'expert'=16] {'pipe'}, dimensions={1} | all-to-all | bytes 2752512 | tf_op jit(solution)/shard_map/all_to_all | solution.py:71
  219.3 1.2 reverse.3
  220.5 2.5 copy.69
  223.1 4.6 %all-to-all-start.3 = ((bf16[6,896,128]{2,1,0:T(8,128)(2,1)}), bf16[6,896,128]{2,1,0:T(8,128)(2,1)}, u32[]{:S(2)}, u32[]{:S(2)}) async-start(bf16[6,896,128]{2,1,0:T(8,128)(2,1)} %bitcast.20), calls=%async_computation.3 | async-start | bytes 2752512 | tf_op jit(solution)/shard_map/all_to_all | solution.py:71
  227.7 2.4 squeeze.35
  230.6 3.2 convolution_convert_fusion
  233.8 3.3 reshape.117
  237.1 6.6 %all-to-all-done.3 = bf16[6,896,128]{2,1,0:T(8,128)(2,1)} async-done(((bf16[6,896,128]{2,1,0:T(8,128)(2,1)}), bf16[6,896,128]{2,1,0:T(8,128)(2,1)}, u32[]{:S(2)}, u32[]{:S(2)}) %all-to-all-start.3) | async-done | bytes 1376288 | tf_op jit(solution)/shard_map/all_to_all | solution.py:71
  243.7 8.8 %all-to-all-start = ((bf16[16,12,3584]{2,1,0:T(8,128)(2,1)}), bf16[16,12,3584]{2,1,0:T(8,128)(2,1)}, u32[]{:S(2)}, u32[]{:S(2)}) async-start(bf16[16,12,3584]{2,1,0:T(8,128)(2,1)} %reshape.117), calls=%async_computation | async-start | bytes 3670016 | tf_op jit(solution)/shard_map/all_to_all | solution.py:56
  253.5 1.4 reshape.120
  254.9 39.4 %all-to-all-done = bf16[16,12,3584]{2,1,0:T(8,128)(2,1)} async-done(((bf16[16,12,3584]{2,1,0:T(8,128)(2,1)}), bf16[16,12,3584]{2,1,0:T(8,128)(2,1)}, u32[]{:S(2)}, u32[]{:S(2)}) %all-to-all-start) | async-done | bytes 1376288 | tf_op jit(solution)/shard_map/all_to_all | solution.py:56
  294.3 4.9 %all-to-all-start.1 = ((bf16[16,12,3584]{2,1,0:T(8,128)(2,1)}), bf16[16,12,3584]{2,1,0:T(8,128)(2,1)S(1)}, u32[]{:S(2)}, u32[]{:S(2)}) async-start(bf16[16,12,3584]{2,1,0:T(8,128)(2,1)} %reshape.120), calls=%async_computation.1 | async-start | bytes 3670016 | tf_op jit(solution)/shard_map/all_to_all | solution.py:56
  299.2 1.5 convert_bitcast_fusion
  301.0 1.6 copy-done.2
  305.0 1.8 bitcast_reduce_fusion.1
  306.8 34.2 %all-to-all-done.1 = bf16[16,12,3584]{2,1,0:T(8,128)(2,1)S(1)} async-done(((bf16[16,12,3584]{2,1,0:T(8,128)(2,1)}), bf16[16,12,3584]{2,1,0:T(8,128)(2,1)S(1)}, u32[]{:S(2)}, u32[]{:S(2)}) %all-to-all-start.1) | async-done | bytes 1376288 | tf_op jit(solution)/shard_map/all_to_all | solution.py:56
  (90 shorter events, 30.7 us)
Async XLA Ops:
  0.6 181.2 %copy-start = (bf16[1,3584,128]{2,1,0:T(8,128)(2,1)S(1)}, bf16[1,3584,128]{2,1,0:T(8,128)(2,1)}, u32[]{:S(2)}) copy-start(bf16[1,3584,128]{2,1,0:T(8,128)(2,1)} %param.17) | copy-start | bytes 2752516
  13.6 2.4 copy-start.3
  16.0 5.1 %collective-permute-start = (bf16[3,1,12,3584]{3,2,1,0:T(8,128)(2,1)}, bf16[3,1,12,3584]{3,2,1,0:T(8,128)(2,1)}, u32[]{:S(2)}, u32[]{:S(2)}) collective-permute-start(bf16[3,1,12,3584]{3,2,1,0:T(8,128)(2,1)} %get-tuple-element.51), channel_id=1, source_target_pairs={{0,1},{1,0},{2,3},{3,2},{4,5},{5,4},{6,7},{7,6},{8,9},{9,8},{10,11... | collective-permute-start | bytes 774152 | tf_op jit(solution)/shard_map/ppermute | solution.py:21
  16.7 154.9 %collective-permute-start.14 = (bf16[3,1,12,3584]{3,2,1,0:T(8,128)(2,1)S(1)}, bf16[3,1,12,3584]{3,2,1,0:T(8,128)(2,1)}, u32[]{:S(2)}, u32[]{:S(2)}) collective-permute-start(bf16[3,1,12,3584]{3,2,1,0:T(8,128)(2,1)S(1)} %get-tuple-element.37), channel_id=1, source_target_pairs={{0,15},{1,14},{2,13},{3,12},{4,11},{5,10},{6,9},{7,8},{8,7},{9,6},... | collective-permute-start | bytes 774152 | tf_op jit(solution)/shard_map/ppermute | solution.py:21
  17.8 152.1 %collective-permute-start.13 = (bf16[3,1,12,3584]{3,2,1,0:T(8,128)(2,1)S(1)}, bf16[3,1,12,3584]{3,2,1,0:T(8,128)(2,1)}, u32[]{:S(2)}, u32[]{:S(2)}) collective-permute-start(bf16[3,1,12,3584]{3,2,1,0:T(8,128)(2,1)S(1)} %get-tuple-element.38), channel_id=1, source_target_pairs={{0,14},{1,15},{2,12},{3,13},{4,10},{5,11},{6,8},{7,9},{8,6},{9,7},... | collective-permute-start | bytes 774152 | tf_op jit(solution)/shard_map/ppermute | solution.py:21
  18.9 149.2 %collective-permute-start.12 = (bf16[3,1,12,3584]{3,2,1,0:T(8,128)(2,1)S(1)}, bf16[3,1,12,3584]{3,2,1,0:T(8,128)(2,1)}, u32[]{:S(2)}, u32[]{:S(2)}) collective-permute-start(bf16[3,1,12,3584]{3,2,1,0:T(8,128)(2,1)S(1)} %get-tuple-element.39), channel_id=1, source_target_pairs={{0,13},{1,12},{2,15},{3,14},{4,9},{5,8},{6,11},{7,10},{8,5},{9,4},... | collective-permute-start | bytes 774152 | tf_op jit(solution)/shard_map/ppermute | solution.py:21
  20.9 145.5 %collective-permute-start.11 = (bf16[3,1,12,3584]{3,2,1,0:T(8,128)(2,1)S(1)}, bf16[3,1,12,3584]{3,2,1,0:T(8,128)(2,1)}, u32[]{:S(2)}, u32[]{:S(2)}) collective-permute-start(bf16[3,1,12,3584]{3,2,1,0:T(8,128)(2,1)S(1)} %get-tuple-element.40), channel_id=1, source_target_pairs={{0,12},{1,13},{2,14},{3,15},{4,8},{5,9},{6,10},{7,11},{8,4},{9,5},... | collective-permute-start | bytes 774152 | tf_op jit(solution)/shard_map/ppermute | solution.py:21
  21.1 53.1 %copy-start.9 = (bf16[3,1,12,3584]{3,2,1,0:T(8,128)(2,1)S(1)}, bf16[3,1,12,3584]{3,2,1,0:T(8,128)(2,1)}, u32[]{:S(2)}) copy-start(bf16[3,1,12,3584]{3,2,1,0:T(8,128)(2,1)} %get-tuple-element.46) | copy-start | bytes 774148
  21.1 63.7 %copy-start.8 = (bf16[3,1,12,3584]{3,2,1,0:T(8,128)(2,1)S(1)}, bf16[3,1,12,3584]{3,2,1,0:T(8,128)(2,1)}, u32[]{:S(2)}) copy-start(bf16[3,1,12,3584]{3,2,1,0:T(8,128)(2,1)} %get-tuple-element.45) | copy-start | bytes 774148
  21.1 75.2 %copy-start.7 = (bf16[3,1,12,3584]{3,2,1,0:T(8,128)(2,1)S(1)}, bf16[3,1,12,3584]{3,2,1,0:T(8,128)(2,1)}, u32[]{:S(2)}) copy-start(bf16[3,1,12,3584]{3,2,1,0:T(8,128)(2,1)} %get-tuple-element.44) | copy-start | bytes 774148
  21.1 9.8 %collective-permute-start.1 = (bf16[3,1,12,3584]{3,2,1,0:T(8,128)(2,1)}, bf16[3,1,12,3584]{3,2,1,0:T(8,128)(2,1)S(1)}, u32[]{:S(2)}, u32[]{:S(2)}) collective-permute-start(bf16[3,1,12,3584]{3,2,1,0:T(8,128)(2,1)} %get-tuple-element.50), channel_id=1, source_target_pairs={{0,2},{1,3},{2,0},{3,1},{4,6},{5,7},{6,4},{7,5},{8,10},{9,11},{10,... | collective-permute-start | bytes 774152 | tf_op jit(solution)/shard_map/ppermute | solution.py:21
  30.9 10.7 %collective-permute-start.2 = (bf16[3,1,12,3584]{3,2,1,0:T(8,128)(2,1)}, bf16[3,1,12,3584]{3,2,1,0:T(8,128)(2,1)S(1)}, u32[]{:S(2)}, u32[]{:S(2)}) collective-permute-start(bf16[3,1,12,3584]{3,2,1,0:T(8,128)(2,1)} %get-tuple-element.49), channel_id=1, source_target_pairs={{0,3},{1,2},{2,1},{3,0},{4,7},{5,6},{6,5},{7,4},{8,11},{9,10},{10,... | collective-permute-start | bytes 774152 | tf_op jit(solution)/shard_map/ppermute | solution.py:21
  41.6 21.5 %collective-permute-start.3 = (bf16[3,1,12,3584]{3,2,1,0:T(8,128)(2,1)}, bf16[3,1,12,3584]{3,2,1,0:T(8,128)(2,1)S(1)}, u32[]{:S(2)}, u32[]{:S(2)}) collective-permute-start(bf16[3,1,12,3584]{3,2,1,0:T(8,128)(2,1)} %get-tuple-element.48), channel_id=1, source_target_pairs={{0,4},{1,5},{2,6},{3,7},{4,0},{5,1},{6,2},{7,3},{8,12},{9,13},{10,... | collective-permute-start | bytes 774152 | tf_op jit(solution)/shard_map/ppermute | solution.py:21
  63.1 11.1 %collective-permute-start.4 = (bf16[3,1,12,3584]{3,2,1,0:T(8,128)(2,1)}, bf16[3,1,12,3584]{3,2,1,0:T(8,128)(2,1)S(1)}, u32[]{:S(2)}, u32[]{:S(2)}) collective-permute-start(bf16[3,1,12,3584]{3,2,1,0:T(8,128)(2,1)} %get-tuple-element.47), channel_id=1, source_target_pairs={{0,5},{1,4},{2,7},{3,6},{4,1},{5,0},{6,3},{7,2},{8,13},{9,12},{10,... | collective-permute-start | bytes 774152 | tf_op jit(solution)/shard_map/ppermute | solution.py:21
  74.2 10.6 %collective-permute-start.5 = (bf16[3,1,12,3584]{3,2,1,0:T(8,128)(2,1)S(1)}, bf16[3,1,12,3584]{3,2,1,0:T(8,128)(2,1)S(1)}, u32[]{:S(2)}, u32[]{:S(2)}) collective-permute-start(bf16[3,1,12,3584]{3,2,1,0:T(8,128)(2,1)S(1)} %copy-done.9), channel_id=1, source_target_pairs={{0,6},{1,7},{2,4},{3,5},{4,2},{5,3},{6,0},{7,1},{8,14},{9,15},{10,... | collective-permute-start | bytes 774152 | tf_op jit(solution)/shard_map/ppermute | solution.py:21
  84.8 11.5 %collective-permute-start.6 = (bf16[3,1,12,3584]{3,2,1,0:T(8,128)(2,1)S(1)}, bf16[3,1,12,3584]{3,2,1,0:T(8,128)(2,1)S(1)}, u32[]{:S(2)}, u32[]{:S(2)}) collective-permute-start(bf16[3,1,12,3584]{3,2,1,0:T(8,128)(2,1)S(1)} %copy-done.8), channel_id=1, source_target_pairs={{0,7},{1,6},{2,5},{3,4},{4,3},{5,2},{6,1},{7,0},{8,15},{9,14},{10,... | collective-permute-start | bytes 774152 | tf_op jit(solution)/shard_map/ppermute | solution.py:21
  96.2 14.1 %collective-permute-start.7 = (bf16[3,1,12,3584]{3,2,1,0:T(8,128)(2,1)S(1)}, bf16[3,1,12,3584]{3,2,1,0:T(8,128)(2,1)S(1)}, u32[]{:S(2)}, u32[]{:S(2)}) collective-permute-start(bf16[3,1,12,3584]{3,2,1,0:T(8,128)(2,1)S(1)} %copy-done.7), channel_id=1, source_target_pairs={{0,8},{1,9},{2,10},{3,11},{4,12},{5,13},{6,14},{7,15},{8,0},{9,1},... | collective-permute-start | bytes 774152 | tf_op jit(solution)/shard_map/ppermute | solution.py:21
  110.3 18.9 %collective-permute-start.8 = (bf16[3,1,12,3584]{3,2,1,0:T(8,128)(2,1)S(1)}, bf16[3,1,12,3584]{3,2,1,0:T(8,128)(2,1)S(1)}, u32[]{:S(2)}, u32[]{:S(2)}) collective-permute-start(bf16[3,1,12,3584]{3,2,1,0:T(8,128)(2,1)S(1)} %get-tuple-element.43), channel_id=1, source_target_pairs={{0,9},{1,8},{2,11},{3,10},{4,13},{5,12},{6,15},{7,14},{8,1},{9,0},... | collective-permute-start | bytes 774152 | tf_op jit(solution)/shard_map/ppermute | solution.py:21
  129.2 18.9 %collective-permute-start.9 = (bf16[3,1,12,3584]{3,2,1,0:T(8,128)(2,1)S(1)}, bf16[3,1,12,3584]{3,2,1,0:T(8,128)(2,1)S(1)}, u32[]{:S(2)}, u32[]{:S(2)}) collective-permute-start(bf16[3,1,12,3584]{3,2,1,0:T(8,128)(2,1)S(1)} %get-tuple-element.42), channel_id=1, source_target_pairs={{0,10},{1,11},{2,8},{3,9},{4,14},{5,15},{6,12},{7,13},{8,2},{9,3},... | collective-permute-start | bytes 774152 | tf_op jit(solution)/shard_map/ppermute | solution.py:21
  148.1 17.5 %collective-permute-start.10 = (bf16[3,1,12,3584]{3,2,1,0:T(8,128)(2,1)S(1)}, bf16[3,1,12,3584]{3,2,1,0:T(8,128)(2,1)S(1)}, u32[]{:S(2)}, u32[]{:S(2)}) collective-permute-start(bf16[3,1,12,3584]{3,2,1,0:T(8,128)(2,1)S(1)} %get-tuple-element.41), channel_id=1, source_target_pairs={{0,11},{1,10},{2,9},{3,8},{4,15},{5,14},{6,13},{7,12},{8,3},{9,2},... | collective-permute-start | bytes 774152 | tf_op jit(solution)/shard_map/ppermute | solution.py:21
  179.4 3.0 copy-start.4
  181.8 1.3 copy-start.5
  182.4 1.5 copy-start.6
  186.1 8.7 %copy-start.1 = (bf16[3,3584,128]{2,1,0:T(8,128)(2,1)}, bf16[3,3584,128]{2,1,0:T(8,128)(2,1)S(1)}, u32[]{:S(2)}) copy-start(bf16[3,3584,128]{2,1,0:T(8,128)(2,1)S(1)} %pad_maximum_fusion) | copy-start | bytes 8257540
  223.1 20.6 %all-to-all-start.3 = ((bf16[6,896,128]{2,1,0:T(8,128)(2,1)}), bf16[6,896,128]{2,1,0:T(8,128)(2,1)}, u32[]{:S(2)}, u32[]{:S(2)}) async-start(bf16[6,896,128]{2,1,0:T(8,128)(2,1)} %bitcast.20), calls=%async_computation.3 | async-start | bytes 2752512 | tf_op jit(solution)/shard_map/all_to_all | solution.py:71
  243.7 50.7 %all-to-all-start = ((bf16[16,12,3584]{2,1,0:T(8,128)(2,1)}), bf16[16,12,3584]{2,1,0:T(8,128)(2,1)}, u32[]{:S(2)}, u32[]{:S(2)}) async-start(bf16[16,12,3584]{2,1,0:T(8,128)(2,1)} %reshape.117), calls=%async_computation | async-start | bytes 3670016 | tf_op jit(solution)/shard_map/all_to_all | solution.py:56
  294.3 46.7 %all-to-all-start.1 = ((bf16[16,12,3584]{2,1,0:T(8,128)(2,1)}), bf16[16,12,3584]{2,1,0:T(8,128)(2,1)S(1)}, u32[]{:S(2)}, u32[]{:S(2)}) async-start(bf16[16,12,3584]{2,1,0:T(8,128)(2,1)} %reshape.120), calls=%async_computation.1 | async-start | bytes 3670016 | tf_op jit(solution)/shard_map/all_to_all | solution.py:56
  300.8 1.8 copy-start.2
